TPU v7x, 32 devices: a whole 2x2x4 slice. The times are simulated.
32 devices in a mesh: site: 8 (over y, x, core), scen: 4 (over z).
Axes of the slice: x: 2, y: 2, z: 4, core: 2. Of those that a mesh axis runs over, the one named last changes fastest.
Arguments:
- normals: bfloat16 [20480, 1344], P('site', 'scen'), may hold values from -6 to 6
- pattern: int32 [32, 40], replicated, may hold values from 0 to 79, as said below
- factor: bfloat16 [32, 40, 256, 256], P('site', None, 'scen'), may hold values from -0.0625 to 0.0625
- temporal: bfloat16 [168, 168], replicated, may hold values from -0.5 to 0.5
- capacity: float32 [8192], P('site'), may hold values from 0.05 to 0.4
- spread: float32 [8192], P('site'), may hold values from 0.2 to 0.8
- bus_map: int32 [8192], replicated, may hold values from 0 to 511
Outputs:
- bus_power: float32 [512, 1344], P('site', 'scen')
Inputs may be any that keep to these rules, and one draw needn't show every extreme that they name: `pattern`: each block row names 40 different column blocks. The 4 block rows of one index of site (rows k * 4 to (k + 1) * 4 - 1) name at most 5 different column blocks among those held by any one index of site (blocks j * 10 to (j + 1) * 10 - 1), and exactly 5 among those held by index k itself.
All inputs are finite; a program needn't handle non-finite values.
Results may differ from a plain program's by a relative error of at most 0.0013.
Values may be sent and summed in bfloat16 or wider, within the bound.
A program may use at most 192 MiB of HBM per device.

v0:
```python
import jax
import jax.numpy as jnp
from jax import lax
from jax.sharding import PartitionSpec as P

BLK = 256
HOURS = 168
NZ = 40
MAX_COLUMN_BLOCKS = 5
RB_DEV = 4
BUS_DEV = 64


def shards(normals, pattern, factor, temporal, capacity, spread, bus_map):
    own_index = lax.axis_index("site")
    site_count = lax.axis_size("site")
    row_width = normals.shape[1]
    scen_here = row_width // HOURS
    local_blocks = normals.reshape(-1, BLK, row_width)
    block_count = local_blocks.shape[0]
    all_blocks = block_count * site_count
    my_columns = lax.dynamic_slice_in_dim(pattern, own_index * RB_DEV, RB_DEV, 0).reshape(-1)
    block_ids = jnp.arange(all_blocks, dtype=jnp.int32)
    wanted = pattern.reshape(site_count, -1)
    needed = jnp.any(wanted[:, :, None] == block_ids[None, None, :], axis=1)
    owned_need = lax.dynamic_slice_in_dim(needed, own_index * block_count, block_count, 1).astype(
        jnp.int32
    )
    slot_rank = jnp.cumsum(owned_need, axis=1) - 1
    slot_ids = jnp.arange(MAX_COLUMN_BLOCKS, dtype=jnp.int32)
    chosen = (owned_need[:, None, :] == 1) & (slot_rank[:, None, :] == slot_ids[None, :, None])
    local_ids = jnp.arange(block_count, dtype=jnp.int32)
    block_index = jnp.sum(jnp.where(chosen, local_ids[None, None, :], 0), axis=2)
    present = jnp.any(chosen, axis=2)
    outgoing = jnp.where(
        present[:, :, None, None], local_blocks[block_index], jnp.zeros((), normals.dtype)
    )
    arrived = lax.all_to_all(outgoing, "site", split_axis=0, concat_axis=0, tiled=True)
    my_need = lax.dynamic_index_in_dim(needed, own_index, 0, keepdims=False).astype(jnp.int32)
    my_rank = (jnp.cumsum(my_need.reshape(site_count, block_count), axis=1) - 1).reshape(-1)
    slot_of = my_columns // block_count * MAX_COLUMN_BLOCKS + my_rank[my_columns]
    picked = jnp.take(
        arrived.reshape(site_count * MAX_COLUMN_BLOCKS, BLK, row_width), slot_of, axis=0
    )
    picked = picked.reshape(RB_DEV, NZ, BLK, row_width)
    capacity_rows = capacity.reshape(RB_DEV, BLK)
    spread_rows = spread.reshape(RB_DEV, BLK)
    portion = lax.all_gather(factor, "scen", axis=2, tiled=True)
    height = portion.shape[2]
    spatial = jnp.einsum(
        "ktij,ktjw->kiw", portion, picked, preferred_element_type=jnp.float32
    ).astype(jnp.bfloat16)
    hourly = spatial.reshape(RB_DEV, height, scen_here, HOURS)
    weather = jnp.einsum("kpsg,hg->kpsh", hourly, temporal, preferred_element_type=jnp.float32)
    scale_part = capacity_rows[:, :, None, None]
    spread_part = spread_rows[:, :, None, None]
    values = scale_part * jnp.exp(spread_part * weather - 0.5 * spread_part * spread_part)
    injected = (
        values.astype(jnp.bfloat16)
        .reshape(RB_DEV, height, row_width)
        .reshape(RB_DEV * BLK, row_width)
    )
    bus_ids = own_index * BUS_DEV + jnp.arange(BUS_DEV, dtype=jnp.int32)
    onehot_rows = (bus_map[None, :] == bus_ids[:, None]).astype(jnp.bfloat16)
    return jnp.dot(
        onehot_rows,
        lax.all_gather(injected, "site", axis=0, tiled=True),
        preferred_element_type=jnp.float32,
    )


def solution(mesh):
    placed = (P("site", "scen"), P(), P("site", None, "scen", None), P(), P("site"), P("site"), P())
    return jax.shard_map(
        shards, mesh=mesh, in_specs=placed, out_specs=P("site", "scen"), check_vma=False
    )
```

profile of v0, /device:TPU:0, one launch (start us, length us, event | category | flops | bytes accessed | tf_op | source)
XLA Modules:
  0.0 440.7 jit_solution(17273901269101868076)
XLA Ops:
  6.5 0.7 all-gather.3.cloned.1.call-update
  7.3 0.8 eq.51
  8.1 0.3 fusion.18
  8.4 0.2 reduce_window_sum.18
  8.6 0.2 select_reduce_fusion
  8.9 3.9 copy.12
  12.8 2.8 copy.14
  15.6 0.2 fusion.21
  15.9 6.4 %gather_fusion.1 = bf16[40,256,336]{1,2,0:T(8,128)(2,1)} fusion(bf16[10,256,336]{1,2,0:T(8,128)(2,1)S(1)} %copy.14, s32[1024]{0:T(1024)S(1)} %pad_clamp_fusion.1), kind=kCustom, calls=%fused_computation.1 | custom fusion | bytes 13762720 | tf_op jit(solution)/shard_map/gather | solution.py:36
  22.3 7.8 %broadcast_select_fusion = bf16[8,5,256,336]{2,3,1,0:T(8,128)(2,1)} fusion(bf16[8,5,256,336]{2,3,1,0:T(8,128)(2,1)} %bitcast.33, pred[8,5]{1,0:T(8,128)(4,1)S(1)} %copy.11), kind=kLoop, calls=%fused_computation.7 | loop fusion | flops 3440640 | bytes 13762600 | tf_op jit(solution)/shard_map/jit(_where)/select_n | solution.py:35
  30.1 5.1 %all-to-all-start = ((bf16[8,5,256,336]{2,3,1,0:T(8,128)(2,1)}), bf16[8,5,256,336]{2,3,1,0:T(8,128)(2,1)}, u32[]{:S(2)}, u32[]{:S(2)}) async-start(bf16[8,5,256,336]{2,3,1,0:T(8,128)(2,1)} %broadcast_select_fusion), calls=%async_computation | async-start | bytes 13762560 | tf_op jit(solution)/shard_map/all_to_all | solution.py:38
  35.2 0.7 constant_dynamic-slice_fusion
  36.1 0.2 reduce_window_sum.17
  36.4 1.6 gather_fusion
  38.1 0.7 compare_and_fusion
  38.8 74.7 %all-to-all-done = bf16[8,5,256,336]{2,3,1,0:T(8,128)(2,1)} async-done(((bf16[8,5,256,336]{2,3,1,0:T(8,128)(2,1)}), bf16[8,5,256,336]{2,3,1,0:T(8,128)(2,1)}, u32[]{:S(2)}, u32[]{:S(2)}) %all-to-all-start) | async-done | bytes 6881312 | tf_op jit(solution)/shard_map/all_to_all | solution.py:38
  113.5 15.0 %gather_fusion.2 = bf16[160,256,336]{1,2,0:T(8,128)(2,1)} fusion(bf16[40,256,336]{1,2,0:T(8,128)(2,1)} %bitcast.4, s32[1024]{0:T(1024)S(1)} %pad_clamp_fusion), kind=kCustom, calls=%fused_computation.2 | custom fusion | bytes 55050880 | tf_op jit(solution)/shard_map/jit(_take)/gather | solution.py:42
  128.5 240.0 %all-gather.3.cloned.1.call-done = bf16[4,40,256,256]{3,2,1,0:T(8,128)(2,1)} async-done(((bf16[4,40,64,256]{3,2,1,0:T(8,128)(2,1)}), bf16[4,40,256,256]{3,2,1,0:T(8,128)(2,1)}) %all-gather.3.cloned.1.call-update) | async-done | bytes 20971536 | tf_op jit(solution)/shard_map/all_gather | solution.py:48
  368.5 17.8 %fusion.13 = bf16[4,336,256]{2,1,0:T(8,128)(2,1)S(1)} fusion(bf16[4,40,256,256]{3,2,1,0:T(8,128)(2,1)} %all-gather.3.cloned.1.call-done, bf16[4,40,256,336]{2,3,1,0:T(8,128)(2,1)} %bitcast.32, pred[4,40]{1,0:T(4,128)(4,1)S(1)} %compare_and_fusion), kind=kOutput, calls=%fused_computation.16 | convolution fusion | flops 7060537344 | bytes 49184928 | tf_op jit(solution)/shard_map/ktij,ktjw->kiw/dot_general | solution.py:50
  386.3 0.4 fusion.12
  386.7 0.4 copy.15
  387.1 1.0 copy.18
  388.2 40.8 %all-gather.5.cloned.1.call-done = bf16[8192,336]{0,1:T(8,128)(2,1)} async-done(((bf16[1024,336]{0,1:T(8,128)(2,1)}), bf16[8192,336]{0,1:T(8,128)(2,1)}) %all-gather.5.cloned.1.call-update) | async-done | bytes 5505040 | tf_op jit(solution)/shard_map/all_gather | solution.py:67
  429.0 4.9 %fusion.4 = f32[64,336]{1,0:T(8,128)} fusion(bf16[8192,336]{0,1:T(8,128)(2,1)} %all-gather.5.cloned.1.call-done, s32[8192]{0:T(1024)S(1)} %copy-done.1, s32[64]{0:T(128)S(1)} %iota_add_fusion), kind=kOutput, calls=%fused_computation.8 | convolution fusion | flops 352845824 | bytes 5624064 | tf_op jit(solution)/shard_map/dot_general | solution.py:65
  (32 shorter events, 0.8 us)
Async XLA Ops:
  6.5 379.8 %copy-start = (bf16[168,168]{1,0:T(8,128)(2,1)S(1)}, bf16[168,168]{1,0:T(8,128)(2,1)}, u32[]{:S(2)}) copy-start(bf16[168,168]{1,0:T(8,128)(2,1)} %param.10) | copy-start | bytes 169348
  6.5 362.0 %all-gather.3.cloned.1.call-start = ((), (), s32[]{:S(2)}) async-start(), calls=%async_computation.1 | async-start | bytes 26214400 | tf_op jit(solution)/shard_map/all_gather | solution.py:48
  30.1 7.9 %copy-start.2 = (f32[1024]{0:T(1024)S(1)}, f32[1024]{0:T(1024)}, u32[]{:S(2)}) copy-start(f32[1024]{0:T(1024)} %param.12) | copy-start | bytes 12292
  30.1 7.9 %copy-start.3 = (f32[1024]{0:T(1024)S(1)}, f32[1024]{0:T(1024)}, u32[]{:S(2)}) copy-start(f32[1024]{0:T(1024)} %param.11) | copy-start | bytes 12292
  30.1 83.4 %all-to-all-start = ((bf16[8,5,256,336]{2,3,1,0:T(8,128)(2,1)}), bf16[8,5,256,336]{2,3,1,0:T(8,128)(2,1)}, u32[]{:S(2)}, u32[]{:S(2)}) async-start(bf16[8,5,256,336]{2,3,1,0:T(8,128)(2,1)} %broadcast_select_fusion), calls=%async_computation | async-start | bytes 13762560 | tf_op jit(solution)/shard_map/all_to_all | solution.py:38
  35.2 393.8 %all-gather.5.cloned.1.call-start = ((), (), s32[]{:S(2)}) async-start(), calls=%async_computation.2 | async-start | bytes 6193152 | tf_op jit(solution)/shard_map/all_gather | solution.py:67
  368.5 60.5 %copy-start.1 = (s32[8192]{0:T(1024)S(1)}, s32[8192]{0:T(1024)}, u32[]{:S(2)}) copy-start(s32[8192]{0:T(1024)} %param.13) | copy-start | bytes 98308
Sparse Core Ops, SparseCore 0:
  8.9 359.5 all-gather.2
  388.3 40.6 all-gather.4
where the time goes:
time: 441 us
  waiting for transfers between devices  356 us (81%)
  local copies, waits for them, and re-layouts  33.1 us (8%)
  matrix products  23.1 us (5%)
  between operations  13.5 us (3%)
  other arithmetic  9.61 us (2%)
  starting transfers between devices  5.11 us (1%)
    all_gather x1, waiting for transfers between devices, shards(): portion = lax.all_gather(factor, 'scen', axis=2, tiled=True)  240 us
    all_to_all x1, waiting for transfers between devices, shards(): lax.all_to_all(outgoing, 'site', split_axis=0, concat_axis=0, tiled=True)  74.7 us
    all_gather x1, waiting for transfers between devices, shards(): lax.all_gather(injected, 'site', axis=0, tiled=True)  40.8 us
    dot_general x1, matrix products, shards(): jnp.einsum('ktij,ktjw->kiw', portion, picked, preferred_element_type=jnp....  17.8 us
    gather x1, local copies, waits for them, and re-layouts, shards(): jnp.take(arrived.reshape(site_count * MAX_COLUMN_BLOCKS, BLK, row_width),...  15 us
  transfers between devices with their start and end apart: 3, of which 3 were waited for; matrix products, arithmetic and copies ran while one was open for 9% of the time, Pallas kernels for 0%

commit v1 on v0

--- a/solution.py
+++ b/solution.py
@@ -45,7 +45,7 @@
     picked = picked.reshape(RB_DEV, NZ, BLK, row_width)
     capacity_rows = capacity.reshape(RB_DEV, BLK)
     spread_rows = spread.reshape(RB_DEV, BLK)
-    portion = lax.all_gather(factor, "scen", axis=2, tiled=True)
+    portion = jnp.concatenate(lax.all_gather(factor, "scen"), axis=2)
     height = portion.shape[2]
     spatial = jnp.einsum(
         "ktij,ktjw->kiw", portion, picked, preferred_element_type=jnp.float32

time: 441 us -> 459 us (1.041)
  local copies, waits for them, and re-layouts: 33.1 us -> 49.2 us
    all_gather x0 -> x1, local copies, waits for them, and re-layouts: none -> 17.6 us  [shards(): portion = jnp.concatenate(lax.all_gather(factor, 'scen'), axis=2)]
where the time goes in v1:
time: 459 us; the launch traced here: 458 us
  waiting for transfers between devices  358 us (78%)
  local copies, waits for them, and re-layouts  49.2 us (11%)
  matrix products  23.2 us (5%)
  between operations  13.5 us (3%)
  other arithmetic  8.98 us (2%)
  starting transfers between devices  5.36 us (1%)
    all_gather x1, waiting for transfers between devices, shards(): portion = jnp.concatenate(lax.all_gather(factor, 'scen'), axis=2)  241 us
    all_to_all x1, waiting for transfers between devices, shards(): lax.all_to_all(outgoing, 'site', split_axis=0, concat_axis=0, tiled=True)  76.1 us
    all_gather x1, waiting for transfers between devices, shards(): lax.all_gather(injected, 'site', axis=0, tiled=True)  40.8 us
    dot_general x1, matrix products, shards(): jnp.einsum('ktij,ktjw->kiw', portion, picked, preferred_element_type=jnp....  17.8 us
    all_gather x1, local copies, waits for them, and re-layouts, shards(): portion = jnp.concatenate(lax.all_gather(factor, 'scen'), axis=2)  17.6 us
    gather x1, local copies, waits for them, and re-layouts, shards(): jnp.take(arrived.reshape(site_count * MAX_COLUMN_BLOCKS, BLK, row_width),...  15 us
  transfers between devices with their start and end apart: 3, of which 3 were waited for; matrix products, arithmetic and copies ran while one was open for 9% of the time, Pallas kernels for 0%

profile of v1, /device:TPU:0, one launch (start us, length us, event | category | flops | bytes accessed | tf_op | source)
XLA Modules:
  0.0 458.4 jit_solution(9636435433377339043)
XLA Ops:
  6.5 0.7 all-gather.6.cloned.1.call-update
  7.3 3.9 copy.18
  11.2 2.8 copy.20
  14.0 0.3 fusion.18
  14.4 0.2 reduce_window_sum.18
  14.5 0.2 select_reduce_fusion
  14.9 0.2 fusion.21
  15.1 0.1 copy.17
  15.2 6.3 %gather_fusion.1 = bf16[40,256,336]{1,2,0:T(8,128)(2,1)} fusion(bf16[10,256,336]{1,2,0:T(8,128)(2,1)S(1)} %copy.20, s32[1024]{0:T(1024)S(1)} %pad_clamp_fusion.1), kind=kCustom, calls=%fused_computation.1 | custom fusion | bytes 13762720 | tf_op jit(solution)/shard_map/gather | solution.py:36
  21.5 7.8 %broadcast_select_fusion = bf16[8,5,256,336]{2,3,1,0:T(8,128)(2,1)} fusion(bf16[8,5,256,336]{2,3,1,0:T(8,128)(2,1)} %bitcast.37, pred[8,5]{1,0:T(8,128)(4,1)S(1)} %copy.17), kind=kLoop, calls=%fused_computation.7 | loop fusion | flops 3440640 | bytes 13762600 | tf_op jit(solution)/shard_map/jit(_where)/select_n | solution.py:35
  29.3 5.3 %all-to-all-start = ((bf16[8,5,256,336]{2,3,1,0:T(8,128)(2,1)}), bf16[8,5,256,336]{2,3,1,0:T(8,128)(2,1)}, u32[]{:S(2)}, u32[]{:S(2)}) async-start(bf16[8,5,256,336]{2,3,1,0:T(8,128)(2,1)} %broadcast_select_fusion), calls=%async_computation | async-start | bytes 13762560 | tf_op jit(solution)/shard_map/all_to_all | solution.py:38
  34.8 0.2 reduce_window_sum.17
  35.2 1.6 gather_fusion
  36.7 0.1 gather.17
  36.9 76.1 %all-to-all-done = bf16[8,5,256,336]{2,3,1,0:T(8,128)(2,1)} async-done(((bf16[8,5,256,336]{2,3,1,0:T(8,128)(2,1)}), bf16[8,5,256,336]{2,3,1,0:T(8,128)(2,1)}, u32[]{:S(2)}, u32[]{:S(2)}) %all-to-all-start) | async-done | bytes 6881312 | tf_op jit(solution)/shard_map/all_to_all | solution.py:38
  113.0 15.0 %gather_fusion.2 = bf16[160,256,336]{1,2,0:T(8,128)(2,1)} fusion(bf16[40,256,336]{1,2,0:T(8,128)(2,1)} %bitcast.4, s32[1024]{0:T(1024)S(1)} %pad_clamp_fusion), kind=kCustom, calls=%fused_computation.2 | custom fusion | bytes 55050880 | tf_op jit(solution)/shard_map/jit(_take)/gather | solution.py:42
  128.0 240.5 %all-gather.6.cloned.1.call-done = bf16[16,40,64,256]{3,2,1,0:T(8,128)(2,1)} async-done(((bf16[4,40,64,256]{3,2,1,0:T(8,128)(2,1)}), bf16[16,40,64,256]{3,2,1,0:T(8,128)(2,1)}) %all-gather.6.cloned.1.call-update) | async-done | bytes 20971536 | tf_op jit(solution)/shard_map/all_gather | solution.py:48
  368.5 17.6 %copy.21 = bf16[4,4,40,64,256]{4,3,0,2,1:T(8,128)(2,1)} copy(bf16[4,4,40,64,256]{4,3,2,1,0:T(8,128)(2,1)} %bitcast.38) | data formatting | bytes 41943040 | tf_op jit(solution)/shard_map/all_gather | solution.py:48
  386.1 17.8 %fusion.13 = bf16[4,336,256]{2,1,0:T(8,128)(2,1)S(1)} fusion(bf16[4,40,256,256]{3,2,1,0:T(8,128)(2,1)} %bitcast.39, bf16[4,40,256,336]{2,3,1,0:T(8,128)(2,1)} %bitcast.36, pred[4,40]{1,0:T(4,128)(4,1)S(1)} %compare_and_fusion), kind=kOutput, calls=%fused_computation.16 | convolution fusion | flops 7060537344 | bytes 49184928 | tf_op jit(solution)/shard_map/ktij,ktjw->kiw/dot_general | solution.py:50
  404.0 0.4 fusion.12
  404.4 0.4 copy.22
  404.8 1.0 copy.25
  405.8 40.8 %all-gather.4.cloned.1.call-done = bf16[8192,336]{0,1:T(8,128)(2,1)} async-done(((bf16[1024,336]{0,1:T(8,128)(2,1)}), bf16[8192,336]{0,1:T(8,128)(2,1)}) %all-gather.4.cloned.1.call-update) | async-done | bytes 5505040 | tf_op jit(solution)/shard_map/all_gather | solution.py:67
  446.6 4.9 %fusion.4 = f32[64,336]{1,0:T(8,128)} fusion(bf16[8192,336]{0,1:T(8,128)(2,1)} %all-gather.4.cloned.1.call-done, s32[8192]{0:T(1024)S(1)} %copy-done.1, s32[64]{0:T(128)S(1)} %iota_add_fusion), kind=kOutput, calls=%fused_computation.8 | convolution fusion | flops 352845824 | bytes 5624064 | tf_op jit(solution)/shard_map/dot_general | solution.py:65
  (35 shorter events, 0.8 us)
Async XLA Ops:
  6.5 397.4 %copy-start = (bf16[168,168]{1,0:T(8,128)(2,1)S(1)}, bf16[168,168]{1,0:T(8,128)(2,1)}, u32[]{:S(2)}) copy-start(bf16[168,168]{1,0:T(8,128)(2,1)} %param.10) | copy-start | bytes 169348
  6.5 7.4 %copy-start.2 = (s32[32,40]{1,0:T(8,128)S(1)}, s32[32,40]{1,0:T(8,128)}, u32[]{:S(2)}) copy-start(s32[32,40]{1,0:T(8,128)} %param.8) | copy-start | bytes 15364
  6.5 362.0 %all-gather.6.cloned.1.call-start = ((), (), s32[]{:S(2)}) async-start(), calls=%async_computation.2 | async-start | bytes 26214400 | tf_op jit(solution)/shard_map/all_gather | solution.py:48
  29.3 7.5 %copy-start.3 = (f32[1024]{0:T(1024)S(1)}, f32[1024]{0:T(1024)}, u32[]{:S(2)}) copy-start(f32[1024]{0:T(1024)} %param.12) | copy-start | bytes 12292
  29.3 7.5 %copy-start.4 = (f32[1024]{0:T(1024)S(1)}, f32[1024]{0:T(1024)}, u32[]{:S(2)}) copy-start(f32[1024]{0:T(1024)} %param.11) | copy-start | bytes 12292
  29.3 83.7 %all-to-all-start = ((bf16[8,5,256,336]{2,3,1,0:T(8,128)(2,1)}), bf16[8,5,256,336]{2,3,1,0:T(8,128)(2,1)}, u32[]{:S(2)}, u32[]{:S(2)}) async-start(bf16[8,5,256,336]{2,3,1,0:T(8,128)(2,1)} %broadcast_select_fusion), calls=%async_computation | async-start | bytes 13762560 | tf_op jit(solution)/shard_map/all_to_all | solution.py:38
  34.7 412.0 %all-gather.4.cloned.1.call-start = ((), (), s32[]{:S(2)}) async-start(), calls=%async_computation.1 | async-start | bytes 6193152 | tf_op jit(solution)/shard_map/all_gather | solution.py:67
  386.1 60.5 %copy-start.1 = (s32[8192]{0:T(1024)S(1)}, s32[8192]{0:T(1024)}, u32[]{:S(2)}) copy-start(s32[8192]{0:T(1024)} %param.13) | copy-start | bytes 98308
Sparse Core Ops, SparseCore 0:
  8.9 359.5 all-gather.5
  405.9 40.6 all-gather.3
